TPU v7x, 32 devices: a whole 2x2x4 slice. The times are simulated.
32 devices in a mesh: dp: 8 (over z, x), tensor: 4 (over y, core).
Axes of the slice: x: 2, y: 2, z: 4, core: 2. Of those that a mesh axis runs over, the one named last changes fastest.
Arguments:
- cells_x: bfloat16 [16384, 768], P(('dp', 'tensor')), may hold values from -6 to 6
- cotangent: bfloat16 [16384, 768], P(('dp', 'tensor')), may hold values from -6 to 6
- gene_counts: int32 [8], replicated, may hold values from 300 to 2048, as said below
- slot_cell: int32 [8], P('dp'), may hold values from 0 to 7, each once
- norm_gain: bfloat16 [2, 768], replicated, may hold values from 0.5 to 1.5
- norm_shift: bfloat16 [2, 768], replicated, may hold values from -1 to 1
- out_bias: bfloat16 [2, 768], replicated, may hold values from -1 to 1
- w_qkv: bfloat16 [3, 768, 768], P(None, None, 'tensor'), may hold values from -0.3125 to 0.3125
- qv_bias: bfloat16 [2, 768], P(None, 'tensor'), may hold values from -1.5 to 1.5
- w_out: bfloat16 [768, 768], P('tensor'), may hold values from -1.75 to 1.75
- w_up: bfloat16 [768, 3072], P(None, 'tensor'), may hold values from -0.21875 to 0.21875
- up_bias: bfloat16 [3072], P('tensor'), may hold values from -1.5 to 1.5
- w_down: bfloat16 [3072, 768], P('tensor'), may hold values from -0.109375 to 0.109375
Outputs:
- block_out: bfloat16 [16384, 768], P(('dp', 'tensor'))
- input_grad: bfloat16 [16384, 768], P(('dp', 'tensor'))
- grad_norm_gain: float32 [2, 768], replicated
- grad_norm_shift: float32 [2, 768], replicated
- grad_out_bias: float32 [2, 768], replicated
- grad_qkv: float32 [3, 768, 768], P(None, None, 'tensor')
- grad_qv_bias: float32 [2, 768], P(None, 'tensor')
- grad_w_out: float32 [768, 768], P('tensor')
- grad_w_up: float32 [768, 3072], P(None, 'tensor')
- grad_up_bias: float32 [3072], P('tensor')
- grad_w_down: float32 [3072, 768], P('tensor')
Inputs may be any that keep to these rules, and one draw needn't show every extreme that they name: `gene_counts`: some cell has exactly 2048 expressed genes and some exactly 300. `slot_cell`: every cell is held in exactly one slot.
All inputs are finite; a program needn't handle non-finite values.
Results may differ from a plain program's by a relative error of at most 0.013.
The roundings to bfloat16 on the way count: a program that leaves them out, or rounds other values in their place, can miss the bound.
Values may be sent and summed in bfloat16 or wider, within the bound.
No kernel may reach another device: no remote copies, remote signals or barrier semaphores. Data moves between devices by JAX's collectives and lax.ppermute only.
A program may use at most 128 MiB of HBM per device.

v0:
```python
import jax
import jax.numpy as jnp
from jax import lax
from jax.sharding import PartitionSpec as P

HEAD_DIM = 64
SLOT = 2048
EPSILON = 1e-05
NEGATIVE = -1e30


def exact_gelu(hidden):
    return jax.nn.gelu(hidden, approximate=False)


def normalize(features, gain_row, shift_row):
    row_mean = jnp.mean(features, axis=-1, keepdims=True)
    centered = features - row_mean
    variance = jnp.mean(centered * centered, axis=-1, keepdims=True)
    inverse = lax.rsqrt(variance + EPSILON)
    scaled = centered * inverse
    return (scaled * gain_row.astype(jnp.float32) + shift_row.astype(jnp.float32), scaled, inverse)


def normalize_back(upstream, scaled, inverse, gain_row):
    graded = upstream * gain_row.astype(jnp.float32)
    grad_mean = jnp.mean(graded, axis=-1, keepdims=True)
    cross_mean = jnp.mean(graded * scaled, axis=-1, keepdims=True)
    return (
        inverse * (graded - grad_mean - scaled * cross_mean),
        jnp.sum(upstream * scaled, axis=0),
        jnp.sum(upstream, axis=0),
    )


def contract_last(left, right):
    return lax.dot_general(
        left, right, (((1,), (1,)), ((), ())), preferred_element_type=jnp.float32
    )


def contract_first(left, right):
    return lax.dot_general(
        left, right, (((0,), (0,)), ((), ())), preferred_element_type=jnp.float32
    )


def masked_scores(block_queries, key_heads, live_keys, score_scale):
    scores = (
        jnp.einsum("qhe,khe->hqk", block_queries, key_heads, preferred_element_type=jnp.float32)
        * score_scale
    )
    return jnp.where(live_keys[None, None, :], scores, NEGATIVE)


def attend_cell(query_heads, key_heads, value_heads, live_keys, block_rows):
    score_scale = query_heads.shape[-1] ** (-0.5)

    def one_block(block_index):
        block_queries = lax.dynamic_slice_in_dim(
            query_heads, block_index * block_rows, block_rows, 0
        )
        scores = masked_scores(block_queries, key_heads, live_keys, score_scale)
        row_max = jnp.max(scores, axis=-1, keepdims=True)
        exp_scores = jnp.exp(scores - row_max)
        row_total = jnp.sum(exp_scores, axis=-1, keepdims=True)
        soft_low = (exp_scores / row_total).astype(jnp.bfloat16)
        attended = jnp.einsum(
            "hqk,khe->qhe", soft_low, value_heads, preferred_element_type=jnp.float32
        )
        return (attended, (row_max + jnp.log(row_total))[..., 0])

    attended, log_totals = lax.map(one_block, jnp.arange(query_heads.shape[0] // block_rows))
    return (attended.reshape(query_heads.shape[0], -1), log_totals)


def attend_back(query_heads, key_heads, value_heads, grad_heads, log_totals, live_keys, block_rows):
    score_scale = query_heads.shape[-1] ** (-0.5)
    slot_rows = query_heads.shape[0]

    def one_block(sums_carry, block_index):
        key_sum, value_sum = sums_carry
        first_row = block_index * block_rows
        block_queries = lax.dynamic_slice_in_dim(query_heads, first_row, block_rows, 0)
        block_grads = lax.dynamic_slice_in_dim(grad_heads, first_row, block_rows, 0)
        scores = masked_scores(block_queries, key_heads, live_keys, score_scale)
        softmaxed = jnp.exp(scores - log_totals[block_index][..., None])
        soft_low = softmaxed.astype(jnp.bfloat16)
        prob_grad = jnp.einsum(
            "qhe,khe->hqk", block_grads, value_heads, preferred_element_type=jnp.float32
        )
        row_inner = jnp.sum(softmaxed * prob_grad, axis=-1, keepdims=True)
        score_grad = (score_scale * softmaxed * (prob_grad - row_inner)).astype(jnp.bfloat16)
        query_grad = jnp.einsum(
            "hqk,khe->qhe", score_grad, key_heads, preferred_element_type=jnp.float32
        )
        key_sum = key_sum + jnp.einsum(
            "hqk,qhe->khe", score_grad, block_queries, preferred_element_type=jnp.float32
        )
        value_sum = value_sum + jnp.einsum(
            "hqk,qhe->khe", soft_low, block_grads, preferred_element_type=jnp.float32
        )
        return ((key_sum, value_sum), query_grad)

    zero_heads = jnp.zeros(key_heads.shape, jnp.float32)
    (key_sum, value_sum), query_grad = lax.scan(
        one_block, (zero_heads, zero_heads), jnp.arange(slot_rows // block_rows)
    )
    return (
        query_grad.reshape(slot_rows, -1).astype(jnp.bfloat16),
        key_sum.reshape(slot_rows, -1).astype(jnp.bfloat16),
        value_sum.reshape(slot_rows, -1).astype(jnp.bfloat16),
    )


def per_device(
    cells_x,
    cotangent,
    gene_counts,
    slot_cell,
    norm_gain,
    norm_shift,
    out_bias,
    w_qkv,
    qv_bias,
    w_out,
    w_up,
    up_bias,
    w_down,
):
    row_count = cells_x.shape[0]
    cells_dev = slot_cell.shape[0]
    group_rows = cells_dev * SLOT
    block_rows = min(512, SLOT)
    cell_ids = jnp.arange(gene_counts.shape[0], dtype=jnp.int32)
    lengths = jnp.sum(
        jnp.where(slot_cell[:, None] == cell_ids[None, :], gene_counts[None, :], 0), axis=1
    )
    positions = jnp.arange(SLOT, dtype=jnp.int32)
    live_keys = positions[None, :] < lengths[:, None]
    row_index = lax.axis_index("tensor") * row_count + jnp.arange(row_count, dtype=jnp.int32)
    cell_of = row_index // SLOT
    length_of = jnp.sum(
        jnp.where(
            cell_of[:, None] == jnp.arange(cells_dev, dtype=jnp.int32)[None, :], lengths[None, :], 0
        ),
        axis=1,
    )
    live_rows = row_index % SLOT < length_of
    inputs = cells_x.astype(jnp.float32)
    normed_in, scaled_in, inverse_in = normalize(inputs, norm_gain[0], norm_shift[0])
    gathered_in = lax.all_gather(normed_in.astype(jnp.bfloat16), "tensor", axis=0, tiled=True)
    bias_rows = jnp.stack([qv_bias[0], jnp.zeros_like(qv_bias[0]), qv_bias[1]]).astype(jnp.float32)
    projected = jnp.einsum("rd,sdc->src", gathered_in, w_qkv, preferred_element_type=jnp.float32)
    projected = (projected + bias_rows[:, None, :]).astype(jnp.bfloat16)
    heads_local = projected.shape[2] // HEAD_DIM
    head_parts = projected.reshape(3, cells_dev, SLOT, heads_local, HEAD_DIM)
    attended, log_totals = lax.map(
        lambda packed: attend_cell(packed[0], packed[1], packed[2], packed[3], block_rows),
        (head_parts[0], head_parts[1], head_parts[2], live_keys),
    )
    attended_low = attended.reshape(group_rows, -1).astype(jnp.bfloat16)
    attn_sum = lax.psum_scatter(
        jnp.dot(attended_low, w_out, preferred_element_type=jnp.float32),
        "tensor",
        scatter_dimension=0,
        tiled=True,
    )
    middle = inputs + attn_sum + out_bias[0].astype(jnp.float32)
    normed_mid, scaled_mid, inverse_mid = normalize(middle, norm_gain[1], norm_shift[1])
    normed_mid_low = normed_mid.astype(jnp.bfloat16)
    up_full, bias_full, down_full = (w_up, up_bias, w_down)
    ffn_rows = lax.all_gather(normed_mid_low, "tensor", axis=0, tiled=True)
    hidden = jnp.dot(ffn_rows, up_full, preferred_element_type=jnp.float32) + bias_full.astype(
        jnp.float32
    )
    active, gelu_back = jax.vjp(exact_gelu, hidden)
    active_low = active.astype(jnp.bfloat16)
    branch = lax.psum_scatter(
        jnp.dot(active_low, w_down, preferred_element_type=jnp.float32).astype(jnp.bfloat16),
        "tensor",
        scatter_dimension=0,
        tiled=True,
    ).astype(jnp.float32)
    output = jnp.where(live_rows[:, None], middle + branch + out_bias[1].astype(jnp.float32), 0.0)
    block_out = output.astype(jnp.bfloat16)
    out_grad = jnp.where(live_rows[:, None], cotangent, jnp.zeros_like(cotangent))
    grad_rows = lax.all_gather(out_grad, "tensor", axis=0, tiled=True)
    hidden_grad = gelu_back(contract_last(grad_rows, down_full))[0].astype(jnp.bfloat16)
    down_grad = contract_first(active_low, grad_rows)
    up_grad = contract_first(ffn_rows, hidden_grad)
    up_bias_grad = jnp.sum(hidden_grad, axis=0, dtype=jnp.float32)
    mid_norm_grad = lax.psum_scatter(
        contract_last(hidden_grad, w_up), "tensor", scatter_dimension=0, tiled=True
    )
    mid_back, gain_mid, shift_mid = normalize_back(
        mid_norm_grad, scaled_mid, inverse_mid, norm_gain[1]
    )
    middle_grad = out_grad.astype(jnp.float32) + mid_back
    middle_rows = lax.all_gather(middle_grad.astype(jnp.bfloat16), "tensor", axis=0, tiled=True)
    attended_grad = contract_last(middle_rows, w_out).astype(jnp.bfloat16)
    out_weight_grad = contract_first(attended_low, middle_rows)
    grad_heads = attended_grad.reshape(cells_dev, SLOT, heads_local, HEAD_DIM)
    query_grad, key_grad, value_grad = lax.map(
        lambda packed: attend_back(
            packed[0], packed[1], packed[2], packed[3], packed[4], packed[5], block_rows
        ),
        (head_parts[0], head_parts[1], head_parts[2], grad_heads, log_totals, live_keys),
    )
    qkv_grad = jnp.stack([query_grad, key_grad, value_grad]).reshape(3, group_rows, -1)
    qkv_weight_grad = jnp.einsum(
        "src,rd->sdc", qkv_grad, gathered_in, preferred_element_type=jnp.float32
    )
    qv_bias_grad = jnp.stack(
        [
            jnp.sum(qkv_grad[0], axis=0, dtype=jnp.float32),
            jnp.sum(qkv_grad[2], axis=0, dtype=jnp.float32),
        ]
    )
    in_norm_grad = lax.psum_scatter(
        jnp.einsum("src,sdc->rd", qkv_grad, w_qkv, preferred_element_type=jnp.float32),
        "tensor",
        scatter_dimension=0,
        tiled=True,
    )
    in_back, gain_in, shift_in = normalize_back(in_norm_grad, scaled_in, inverse_in, norm_gain[0])
    input_grad = (middle_grad + in_back).astype(jnp.bfloat16)
    gain_grad, shift_grad, bias_grad = lax.psum(
        (
            jnp.stack([gain_in, gain_mid]),
            jnp.stack([shift_in, shift_mid]),
            jnp.stack([jnp.sum(middle_grad, axis=0), jnp.sum(out_grad, axis=0, dtype=jnp.float32)]),
        ),
        "tensor",
    )
    (
        qkv_weight_grad,
        qv_bias_grad,
        out_weight_grad,
        up_grad,
        up_bias_grad,
        down_grad,
        gain_grad,
        shift_grad,
        bias_grad,
    ) = lax.psum(
        (
            qkv_weight_grad,
            qv_bias_grad,
            out_weight_grad,
            up_grad,
            up_bias_grad,
            down_grad,
            gain_grad,
            shift_grad,
            bias_grad,
        ),
        "dp",
    )
    return (
        block_out,
        input_grad,
        gain_grad,
        shift_grad,
        bias_grad,
        qkv_weight_grad,
        qv_bias_grad,
        out_weight_grad,
        up_grad,
        up_bias_grad,
        down_grad,
    )


def solution(mesh):
    return jax.shard_map(
        per_device,
        mesh=mesh,
        in_specs=(
            P(("dp", "tensor"), None),
            P(("dp", "tensor"), None),
            P(),
            P("dp"),
            P(),
            P(),
            P(),
            P(None, None, "tensor"),
            P(None, "tensor"),
            P("tensor", None),
            P(None, "tensor"),
            P("tensor"),
            P("tensor", None),
        ),
        out_specs=(
            P(("dp", "tensor"), None),
            P(("dp", "tensor"), None),
            P(),
            P(),
            P(),
            P(None, None, "tensor"),
            P(None, "tensor"),
            P("tensor", None),
            P(None, "tensor"),
            P("tensor"),
            P("tensor", None),
        ),
        check_vma=False,
    )
```

profile of v0, /device:TPU:0, one launch (start us, length us, event | category | flops | bytes accessed | tf_op | source)
XLA Modules:
  0.0 833.0 jit_solution(6018540514751062280)
XLA Ops:
  15.0 29.9 %all-gather.5.cloned.1.call-done = bf16[2048,768]{1,0:T(8,128)(2,1)} async-done(((bf16[512,768]{1,0:T(8,128)(2,1)}), bf16[2048,768]{1,0:T(8,128)(2,1)}) %all-gather.5.cloned.1.call-update) | async-done | bytes 3145744 | tf_op jit(solution)/shard_map/all_gather | solution.py:152
  50.3 45.2 %while.48 = (s32[]{:T(128)}, bf16[4,512,3,64]{1,3,2,0:T(8,128)(2,1)}, f32[4,3,512]{2,1,0:T(4,128)}, s32[4]{0:T(128)S(1)}, bf16[2048,3,64]{0,2,1:T(8,128)(2,1)S(1...) while((s32[]{:T(128)}, ...), condition=%wide.region_6.7_spmd.clone, body=%wide.region_3.6_spmd.clone.sunk | while | flops 843055616 | bytes 46266624 | solution.py:73
  103.9 57.7 %reduce-scatter.5.cloned.1.call-done = f32[512,768]{1,0:T(8,128)} async-done(((f32[2048,768]{1,0:T(8,128)}), f32[512,768]{1,0:T(8,128)}) %reduce-scatter.5.cloned.1.call-update) | async-done | bytes 1572880 | tf_op jit(solution)/shard_map/reduce_scatter | solution.py:163
  170.4 23.4 %all-gather.7.cloned.1.call-done = bf16[2048,768]{1,0:T(8,128)(2,1)} async-done(((bf16[512,768]{1,0:T(8,128)(2,1)}), bf16[2048,768]{1,0:T(8,128)(2,1)}) %all-gather.7.cloned.1.call-update) | async-done | bytes 3145744 | tf_op jit(solution)/shard_map/all_gather | solution.py:173
  193.8 7.5 fusion.75
  201.3 23.0 %all-gather.9.cloned.1.call-done = bf16[2048,768]{1,0:T(8,128)(2,1)} async-done(((bf16[512,768]{1,0:T(8,128)(2,1)}), bf16[2048,768]{1,0:T(8,128)(2,1)}) %all-gather.9.cloned.1.call-update) | async-done | bytes 3145744 | tf_op jit(solution)/shard_map/all_gather | solution.py:188
  224.3 20.2 %convert_reduce_fusion = (f32[768]{0:T(1024)}, bf16[2048,768]{1,0:T(8,128)(2,1)S(1)}, f32[2048,768]{1,0:T(8,128)}) fusion(f32[2048,768]{1,0:T(8,128)} %fusion.75, f32[768]{0:T(1024)S(1)} %convert_element_type.147, bf16[2048,768]{1,0:T(8,128)(2,1)} %all-gather.9.cloned.1.call-done, bf16[768,768]{1,0:T(8,128)(2,1)S(1)} %copy-done), kind=kOutput, calls=%fused_computation.45 | convolution fusion | flops 2533883136 | bytes 20060160 | tf_op jit(solution)/shard_map/dot_general | solution.py:37
  250.9 5.5 multiply_convert_fusion.1
  262.1 47.7 %reduce-scatter.9.cloned.1.call-done = f32[512,768]{1,0:T(8,128)} async-done(((f32[2048,768]{1,0:T(8,128)}), f32[512,768]{1,0:T(8,128)}) %reduce-scatter.9.cloned.1.call-update) | async-done | bytes 1572880 | tf_op jit(solution)/shard_map/reduce_scatter | solution.py:193
  312.5 37.6 %reduce-scatter.7.cloned.1.call-done = bf16[512,768]{1,0:T(8,128)(2,1)} async-done(((bf16[2048,768]{1,0:T(8,128)(2,1)}), bf16[512,768]{1,0:T(8,128)(2,1)}) %reduce-scatter.7.cloned.1.call-update) | async-done | bytes 786448 | tf_op jit(solution)/shard_map/reduce_scatter | solution.py:179
  356.1 28.4 %all-gather.11.cloned.1.call-done = bf16[2048,768]{1,0:T(8,128)(2,1)} async-done(((bf16[512,768]{1,0:T(8,128)(2,1)}), bf16[2048,768]{1,0:T(8,128)(2,1)}) %all-gather.11.cloned.1.call-update) | async-done | bytes 3145744 | tf_op jit(solution)/shard_map/all_gather | solution.py:200
  389.4 122.9 %while.49 = (s32[]{:T(128)}, f32[2048,3,64]{0,2,1:T(8,128)S(1)}, f32[2048,3,64]{0,2,1:T(8,128)}, bf16[4,512,3,64]{1,3,2,0:T(8,128)(2,1)}, s32[4]{0:T(128)S(1)}, ...) while((s32[]{:T(128)}, f32[2048,3,64]{0,2,1:T(8,128)S(1)}, ...), condition=%wide.region_16.17_spmd.clone, body=%wide.region_14.16_spmd.clone.sunk | while | flops 2065170944 | bytes 129419576 | solution.py:106
  396.6 4.9 fusion.145
  401.5 4.8 multiply_reduce_fusion.7
  406.3 5.3 multiply_convert_fusion.3
  411.7 5.6 fusion.146
  426.8 5.5 fusion.145
  432.4 4.8 multiply_reduce_fusion.7
  437.2 5.3 multiply_convert_fusion.3
  442.5 5.6 fusion.146
  457.7 5.5 fusion.145
  468.1 5.3 multiply_convert_fusion.3
  473.4 5.6 fusion.146
  488.6 5.5 fusion.145
  499.0 5.3 multiply_convert_fusion.3
  504.3 5.6 fusion.146
  516.6 6.0 convolution_bitcast_fusion.2
  522.7 7.1 fusion.78
  543.3 38.4 %reduce-scatter.11.cloned.1.call-done = f32[512,768]{1,0:T(8,128)} async-done(((f32[2048,768]{1,0:T(8,128)}), f32[512,768]{1,0:T(8,128)}) %reduce-scatter.11.cloned.1.call-update) | async-done | bytes 1572880 | tf_op jit(solution)/shard_map/reduce_scatter | solution.py:220
  583.9 10.2 %all-reduce.2 = (f32[2,768]{1,0:T(2,128)S(1)}, f32[2,768]{1,0:T(2,128)S(1)}, f32[2,768]{1,0:T(2,128)S(1)}) all-reduce(f32[2,768]{1,0:T(2,128)S(1)} %pad_maximum_fusion.1, f32[2,768]{1,0:T(2,128)S(1)} %pad_maximum_fusion.2, f32[2,768]{1,0:T(2,128)S(1)} %pad_maximum_fusion.3), channel_id=1, replica_groups=mesh['dp'=8,'tensor'=4] {'tensor'}, use_global_device_ids=true, to_apply=%region_22.23 | all-reduce | flops 4608 | bytes 36864 | tf_op jit(solution)/shard_map/psum | solution.py:228
  594.1 40.2 %all-reduce = (f32[2,768]{1,0:T(2,128)}, f32[2,768]{1,0:T(2,128)}, f32[2,768]{1,0:T(2,128)}, f32[2,192]{1,0:T(2,128)}, f32[768]{0:T(1024)}) all-reduce(f32[2,768]{1,0:T(2,128)S(1)} %get-tuple-element.288, f32[2,768]{1,0:T(2,128)S(1)} %get-tuple-element.289, ...), channel_id=1, replica_groups=mesh['dp'=8,'tensor'=4] {'dp'}, use_global_device_ids=true, to_apply=%region_23.24 | all-reduce | flops 5760 | bytes 46080 | tf_op jit(solution)/shard_map/psum | solution.py:246
  637.1 182.5 %all-reduce.5.cloned.1.call-done = (f32[3,768,192]{1,2,0:T(8,128)}, f32[192,768]{1,0:T(8,128)}, f32[768,768]{1,0:T(8,128)}, f32[768,768]{1,0:T(8,128)}) async-done(((f32[3,768,192]{1,2,0:T(8,128)}, f32[192,768]{1,0:T(8,128)}, f32[768,768]{1,0:T(8,128)}, f32[768,768]{1,0:T(8,128)}), (f32[3,768,192]{1,2,0:T(8,128)}, f32[192,768]{1,0:T(8,128)}, f32[768,768]{1,0:T(8,128)}, ...) | async-done | bytes 7077904 | tf_op jit(solution)/shard_map/psum | solution.py:246
  (245 shorter events, 164.9 us)
Async XLA Ops:
  7.2 217.1 %copy-start = (bf16[768,768]{1,0:T(8,128)(2,1)S(1)}, bf16[768,768]{1,0:T(8,128)(2,1)}, u32[]{:S(2)}) copy-start(bf16[768,768]{1,0:T(8,128)(2,1)} %param.29) | copy-start | bytes 3538948
  7.2 7.7 copy-start.37
  7.2 37.6 %copy-start.44 = (bf16[3,768,192]{1,2,0:T(8,128)(2,1)S(1)}, bf16[3,768,192]{1,2,0:T(8,128)(2,1)}, u32[]{:S(2)}) copy-start(bf16[3,768,192]{1,2,0:T(8,128)(2,1)} %param.24) | copy-start | bytes 2654212
  7.2 37.6 %all-gather.5.cloned.1.call-start = ((), (), s32[]{:S(2)}) async-start(), calls=%async_computation.4 | async-start | bytes 3932160 | tf_op jit(solution)/shard_map/all_gather | solution.py:152
  8.7 40.0 %copy-start.27 = (f32[512]{0:T(512)}, f32[512]{0:T(512)S(1)}, u32[]{:S(2)}) copy-start(f32[512]{0:T(512)S(1)} %broadcast_multiply_fusion.5) | copy-start | bytes 6148
  10.2 38.5 %copy-start.29 = (f32[512]{0:T(512)}, f32[512]{0:T(512)S(1)}, u32[]{:S(2)}) copy-start(f32[512]{0:T(512)S(1)} %add_rsqrt_fusion.1) | copy-start | bytes 6148
  11.1 37.7 %copy-start.25 = (f32[768]{0:T(1024)}, f32[768]{0:T(1024)S(1)}, u32[]{:S(2)}) copy-start(f32[768]{0:T(1024)S(1)} %get-tuple-element.312) | copy-start | bytes 9220
  13.5 148.2 %reduce-scatter.5.cloned.1.call-start = ((), (), s32[]{:S(2)}) async-start(), calls=%async_computation.5 | async-start | bytes 7864320 | tf_op jit(solution)/shard_map/reduce_scatter | solution.py:163
  95.5 7.1 copy-start.3
  95.5 7.1 copy-start.6
  102.7 91.1 %all-gather.7.cloned.1.call-start = ((), (), s32[]{:S(2)}) async-start(), calls=%async_computation.6 | async-start | bytes 3932160 | tf_op jit(solution)/shard_map/all_gather | solution.py:173
  165.1 59.2 %all-gather.9.cloned.1.call-start = ((), (), s32[]{:S(2)}) async-start(), calls=%async_computation.8 | async-start | bytes 3932160 | tf_op jit(solution)/shard_map/all_gather | solution.py:188
  169.2 140.6 %reduce-scatter.9.cloned.1.call-start = ((), (), s32[]{:S(2)}) async-start(), calls=%async_computation.9 | async-start | bytes 7864320 | tf_op jit(solution)/shard_map/reduce_scatter | solution.py:193
  224.3 22.0 %copy-start.43 = (bf16[768,768]{1,0:T(8,128)(2,1)S(1)}, bf16[768,768]{1,0:T(8,128)(2,1)}, u32[]{:S(2)}) copy-start(bf16[768,768]{1,0:T(8,128)(2,1)} %param.27) | copy-start | bytes 3538948
  250.8 99.3 %reduce-scatter.7.cloned.1.call-start = ((), (), s32[]{:S(2)}) async-start(), calls=%async_computation.7 | async-start | bytes 3932160 | tf_op jit(solution)/shard_map/reduce_scatter | solution.py:179
  262.0 88.1 %copy-start.11 = (bf16[512,768]{1,0:T(8,128)(2,1)S(1)}, bf16[512,768]{1,0:T(8,128)(2,1)}, u32[]{:S(2)}) copy-start(bf16[512,768]{1,0:T(8,128)(2,1)} %get-tuple-element.299) | copy-start | bytes 2359300
  262.0 88.1 %copy-start.31 = (f32[768]{0:T(1024)S(1)}, f32[768]{0:T(1024)}, u32[]{:S(2)}) copy-start(f32[768]{0:T(1024)} %get-tuple-element.235) | copy-start | bytes 9220
  262.0 88.1 %copy-start.40 = (pred[512]{0:T(512)(128)(4,1)S(1)}, pred[512]{0:T(512)(128)(4,1)}, u32[]{:S(2)}) copy-start(pred[512]{0:T(512)(128)(4,1)} %copy-done.39) | copy-start | bytes 1540
  262.1 122.5 %all-gather.11.cloned.1.call-start = ((), (), s32[]{:S(2)}) async-start(), calls=%async_computation.10 | async-start | bytes 3932160 | tf_op jit(solution)/shard_map/all_gather | solution.py:200
  353.7 30.8 %copy-start.24 = (bf16[192,768]{1,0:T(8,128)(2,1)S(1)}, bf16[192,768]{1,0:T(8,128)(2,1)}, u32[]{:S(2)}) copy-start(bf16[192,768]{1,0:T(8,128)(2,1)} %param.26) | copy-start | bytes 884740
  355.9 225.8 %reduce-scatter.11.cloned.1.call-start = ((), (), s32[]{:S(2)}) async-start(), calls=%async_computation.11 | async-start | bytes 7864320 | tf_op jit(solution)/shard_map/reduce_scatter | solution.py:220
  356.1 33.3 %copy-start.4 = (bf16[2048,3,64]{0,2,1:T(8,128)(2,1)S(1)}, bf16[2048,3,64]{0,2,1:T(8,128)(2,1)}, u32[]{:S(2)}) copy-start(bf16[2048,3,64]{0,2,1:T(8,128)(2,1)} %copy-done.3) | copy-start | bytes 2359300
  512.4 10.2 %copy-start.14 = (bf16[2048,3,64]{0,2,1:T(8,128)(2,1)}, bf16[2048,3,64]{0,2,1:T(8,128)(2,1)S(1)}, u32[]{:S(2)}) copy-start(bf16[2048,3,64]{0,2,1:T(8,128)(2,1)S(1)} %convert_element_type.158) | copy-start | bytes 2359300
  522.6 297.0 %all-reduce.5.cloned.1.call-start = ((), (), s32[]{:S(2)}) async-start(), calls=%async_computation.12 | async-start | bytes 14155776 | tf_op jit(solution)/shard_map/psum | solution.py:246
  522.7 7.1 copy-start.19
  522.7 7.1 copy-start.42
  541.7 39.9 %copy-start.5 = (bf16[512,768]{1,0:T(8,128)(2,1)S(1)}, bf16[512,768]{1,0:T(8,128)(2,1)}, u32[]{:S(2)}) copy-start(bf16[512,768]{1,0:T(8,128)(2,1)} %param.17) | copy-start | bytes 2359300
  541.8 39.9 %copy-start.26 = (f32[768]{0:T(1024)S(1)}, f32[768]{0:T(1024)}, u32[]{:S(2)}) copy-start(f32[768]{0:T(1024)} %copy-done.25) | copy-start | bytes 9220
  541.8 39.9 %copy-start.28 = (f32[512]{0:T(512)S(1)}, f32[512]{0:T(512)}, u32[]{:S(2)}) copy-start(f32[512]{0:T(512)} %copy-done.27) | copy-start | bytes 6148
  541.8 39.9 %copy-start.30 = (f32[512]{0:T(512)S(1)}, f32[512]{0:T(512)}, u32[]{:S(2)}) copy-start(f32[512]{0:T(512)} %copy-done.29) | copy-start | bytes 6148
  541.8 52.3 %copy-start.38 = (f32[768]{0:T(1024)S(1)}, f32[768]{0:T(1024)}, u32[]{:S(2)}) copy-start(f32[768]{0:T(1024)} %get-tuple-element.291) | copy-start | bytes 9220
  541.8 92.5 %copy-start.8 = (f32[512,768]{1,0:T(8,128)S(1)}, f32[512,768]{1,0:T(8,128)}, u32[]{:S(2)}) copy-start(f32[512,768]{1,0:T(8,128)} %copy-done.7) | copy-start | bytes 4718596
  (33 other events, 80.3 us)
Sparse Core Ops, SparseCore 0:
  13.6 31.2 all-gather.4
  102.8 58.8 reduce-scatter.4
  165.2 28.4 all-gather.6
  195.7 28.4 all-gather.8
  251.0 58.8 reduce-scatter.8
  312.2 37.8 reduce-scatter.6
  356.0 28.4 all-gather.10
  522.7 58.8 reduce-scatter.10
  587.2 232.3 all-reduce.4
where the time goes:
time: 842 us; the launch traced here: 833 us
  waiting for transfers between devices  469 us (56%)
  matrix products  176 us (21%)
  other arithmetic  75.6 us (9%)
  blocking collectives  50.4 us (6%)
  local copies, waits for them, and re-layouts  33 us (4%)
  between operations  15.2 us (2%)
  loops' own time  12.7 us (2%)
    psum x1, waiting for transfers between devices, per_device(): lax.psum((qkv_weight_grad, qv_bias_grad, out_weight_grad, up_grad, up_bia...  182 us
    reduce_scatter x1, waiting for transfers between devices, per_device(): lax.psum_scatter(jnp.dot(attended_low, w_out, preferred_element_type=jnp....  57.7 us
    reduce_scatter x1, waiting for transfers between devices, per_device(): lax.psum_scatter(contract_last(hidden_grad, w_up), 'tensor', scatter_dime...  47.7 us
    psum x1, blocking collectives, per_device(): lax.psum((qkv_weight_grad, qv_bias_grad, out_weight_grad, up_grad, up_bia...  40.2 us
    reduce_scatter x1, waiting for transfers between devices, per_device(): lax.psum_scatter(jnp.einsum('src,sdc->rd', qkv_grad, w_qkv, preferred_ele...  38.4 us
    reduce_scatter x1, waiting for transfers between devices, per_device(): lax.psum_scatter(jnp.dot(active_low, w_down, preferred_element_type=jnp.f...  37.6 us
    all_gather x1, waiting for transfers between devices, per_device(): lax.all_gather(normed_in.astype(jnp.bfloat16), 'tensor', axis=0, tiled=True)  29.9 us
    dot_general x3, matrix products, contract_last(): lax.dot_general(left, right, (((1,), (1,)), ((), ())), preferred_element_...  28.7 us
  transfers between devices with their start and end apart: 9, of which 9 were waited for; matrix products, arithmetic and copies ran while one was open for 6% of the time, Pallas kernels for 0%

commit v1 on v0

--- a/solution.py
+++ b/solution.py
@@ -197,7 +197,24 @@
         mid_norm_grad, scaled_mid, inverse_mid, norm_gain[1]
     )
     middle_grad = out_grad.astype(jnp.float32) + mid_back
-    middle_rows = lax.all_gather(middle_grad.astype(jnp.bfloat16), "tensor", axis=0, tiled=True)
+    value = middle_grad.astype(jnp.bfloat16)
+    devices, mine, rows = (lax.axis_size("tensor"), lax.axis_index("tensor"), value.shape[0])
+    upward = [(i, (i + 1) % devices) for i in range(devices)]
+    backward = [(i, (i - 1) % devices) for i in range(devices)]
+    middle_rows = jnp.zeros((*value.shape[:0], devices * rows, *value.shape[0 + 1 :]), value.dtype)
+    middle_rows = lax.dynamic_update_slice_in_dim(middle_rows, value, mine * rows, axis=0)
+    from_left = from_right = value
+    middle_2 = devices // 2
+    for step in range(1, middle_2 + 1):
+        from_left = lax.ppermute(from_left, "tensor", upward)
+        middle_rows = lax.dynamic_update_slice_in_dim(
+            middle_rows, from_left, (mine - step) % devices * rows, axis=0
+        )
+        if step < devices - middle_2:
+            from_right = lax.ppermute(from_right, "tensor", backward)
+            middle_rows = lax.dynamic_update_slice_in_dim(
+                middle_rows, from_right, (mine + step) % devices * rows, axis=0
+            )
     attended_grad = contract_last(middle_rows, w_out).astype(jnp.bfloat16)
     out_weight_grad = contract_first(attended_low, middle_rows)
     grad_heads = attended_grad.reshape(cells_dev, SLOT, heads_local, HEAD_DIM)

time: 842 us -> 849 us (level)
    all_gather x1 -> x0, waiting for transfers between devices: 28.4 us -> none  [per_device(): lax.all_gather(middle_grad.astype(jnp.bfloat16), 'tensor', axis=0, tiled=...]
    ppermute x0 -> x3, waiting for transfers between devices: none -> 26 us  [the longest x2 26 us: per_device(): from_left = lax.ppermute(from_left, 'tensor', upward)]
    unnamed x93 -> x95, local copies, waits for them, and re-layouts: 17.2 us -> 17.6 us
  transfers between devices with their start and end apart: 9 -> 11, of which waited for: 9 -> 10; matrix products, arithmetic and copies ran while one was open for 6% -> 6% of each run, Pallas kernels for 0% -> 0%
where the time goes in v1:
time: 849 us; the launch traced here: 840 us
  waiting for transfers between devices  466 us (55%)
  matrix products  177 us (21%)
  other arithmetic  75.8 us (9%)
  blocking collectives  50.4 us (6%)
  local copies, waits for them, and re-layouts  38.9 us (5%)
  between operations  15.5 us (2%)
  loops' own time  13.8 us (2%)
    psum x1, waiting for transfers between devices, per_device(): lax.psum((qkv_weight_grad, qv_bias_grad, out_weight_grad, up_grad, up_bia...  182 us
    reduce_scatter x1, waiting for transfers between devices, per_device(): lax.psum_scatter(jnp.dot(attended_low, w_out, preferred_element_type=jnp....  57.7 us
    reduce_scatter x1, waiting for transfers between devices, per_device(): lax.psum_scatter(contract_last(hidden_grad, w_up), 'tensor', scatter_dime...  47.7 us
    psum x1, blocking collectives, per_device(): lax.psum((qkv_weight_grad, qv_bias_grad, out_weight_grad, up_grad, up_bia...  40.2 us
    reduce_scatter x1, waiting for transfers between devices, per_device(): lax.psum_scatter(jnp.einsum('src,sdc->rd', qkv_grad, w_qkv, preferred_ele...  38.2 us
    reduce_scatter x1, waiting for transfers between devices, per_device(): lax.psum_scatter(jnp.dot(active_low, w_down, preferred_element_type=jnp.f...  37.6 us
    all_gather x1, waiting for transfers between devices, per_device(): lax.all_gather(normed_in.astype(jnp.bfloat16), 'tensor', axis=0, tiled=True)  29.9 us
    dot_general x3, matrix products, contract_last(): lax.dot_general(left, right, (((1,), (1,)), ((), ())), preferred_element_...  28.8 us
  transfers between devices with their start and end apart: 11, of which 10 were waited for; matrix products, arithmetic and copies ran while one was open for 6% of the time, Pallas kernels for 0%

profile of v1, /device:TPU:0, one launch (start us, length us, event | category | flops | bytes accessed | tf_op | source)
XLA Modules:
  0.0 839.7 jit_solution(5775325854139061448)
XLA Ops:
  15.0 29.9 %all-gather.4.cloned.1.call-done = bf16[2048,768]{1,0:T(8,128)(2,1)} async-done(((bf16[512,768]{1,0:T(8,128)(2,1)}), bf16[2048,768]{1,0:T(8,128)(2,1)}) %all-gather.4.cloned.1.call-update) | async-done | bytes 3145744 | tf_op jit(solution)/shard_map/all_gather | solution.py:152
  50.3 45.2 %while.48 = (s32[]{:T(128)}, bf16[4,512,3,64]{1,3,2,0:T(8,128)(2,1)}, f32[4,3,512]{2,1,0:T(4,128)}, s32[4]{0:T(128)S(1)}, bf16[2048,3,64]{0,2,1:T(8,128)(2,1)S(1...) while((s32[]{:T(128)}, ...), condition=%wide.region_6.7_spmd.clone, body=%wide.region_3.6_spmd.clone.sunk | while | flops 843055616 | bytes 46266624 | solution.py:73
  103.9 57.7 %reduce-scatter.5.cloned.1.call-done = f32[512,768]{1,0:T(8,128)} async-done(((f32[2048,768]{1,0:T(8,128)}), f32[512,768]{1,0:T(8,128)}) %reduce-scatter.5.cloned.1.call-update) | async-done | bytes 1572880 | tf_op jit(solution)/shard_map/reduce_scatter | solution.py:163
  170.4 23.4 %all-gather.6.cloned.1.call-done = bf16[2048,768]{1,0:T(8,128)(2,1)} async-done(((bf16[512,768]{1,0:T(8,128)(2,1)}), bf16[2048,768]{1,0:T(8,128)(2,1)}) %all-gather.6.cloned.1.call-update) | async-done | bytes 3145744 | tf_op jit(solution)/shard_map/all_gather | solution.py:173
  193.8 7.5 fusion.75
  201.3 23.0 %all-gather.8.cloned.1.call-done = bf16[2048,768]{1,0:T(8,128)(2,1)} async-done(((bf16[512,768]{1,0:T(8,128)(2,1)}), bf16[2048,768]{1,0:T(8,128)(2,1)}) %all-gather.8.cloned.1.call-update) | async-done | bytes 3145744 | tf_op jit(solution)/shard_map/all_gather | solution.py:188
  224.3 20.2 %convert_reduce_fusion = (f32[768]{0:T(1024)}, bf16[2048,768]{1,0:T(8,128)(2,1)S(1)}, f32[2048,768]{1,0:T(8,128)}) fusion(f32[2048,768]{1,0:T(8,128)} %fusion.75, f32[768]{0:T(1024)S(1)} %convert_element_type.147, bf16[2048,768]{1,0:T(8,128)(2,1)} %all-gather.8.cloned.1.call-done, bf16[768,768]{1,0:T(8,128)(2,1)S(1)} %copy-done), kind=kOutput, calls=%fused_computation.45 | convolution fusion | flops 2533883136 | bytes 20060160 | tf_op jit(solution)/shard_map/dot_general | solution.py:37
  250.9 5.5 multiply_convert_fusion.1
  262.1 47.7 %reduce-scatter.9.cloned.1.call-done = f32[512,768]{1,0:T(8,128)} async-done(((f32[2048,768]{1,0:T(8,128)}), f32[512,768]{1,0:T(8,128)}) %reduce-scatter.9.cloned.1.call-update) | async-done | bytes 1572880 | tf_op jit(solution)/shard_map/reduce_scatter | solution.py:193
  312.5 37.6 %reduce-scatter.7.cloned.1.call-done = bf16[512,768]{1,0:T(8,128)(2,1)} async-done(((bf16[2048,768]{1,0:T(8,128)(2,1)}), bf16[512,768]{1,0:T(8,128)(2,1)}) %reduce-scatter.7.cloned.1.call-update) | async-done | bytes 786448 | tf_op jit(solution)/shard_map/reduce_scatter | solution.py:179
  358.5 17.7 %collective-permute-done = bf16[512,768]{1,0:T(8,128)(2,1)S(1)} collective-permute-done((bf16[512,768]{1,0:T(8,128)(2,1)}, bf16[512,768]{1,0:T(8,128)(2,1)S(1)}, u32[]{:S(2)}, u32[]{:S(2)}) %collective-permute-start) | collective-permute-done | bytes 786464 | tf_op jit(solution)/shard_map/ppermute | solution.py:209
  379.5 8.4 collective-permute-done.2
  394.9 124.2 %while.49 = (s32[]{:T(128)}, f32[2048,3,64]{0,2,1:T(8,128)S(1)}, f32[2048,3,64]{0,2,1:T(8,128)}, bf16[4,512,3,64]{1,3,2,0:T(8,128)(2,1)}, s32[4]{0:T(128)S(1)}, ...) while((s32[]{:T(128)}, f32[2048,3,64]{0,2,1:T(8,128)S(1)}, ...), condition=%wide.region_16.17_spmd.clone, body=%wide.region_14.16_spmd.clone.sunk | while | flops 2065170944 | bytes 129419576 | solution.py:106
  402.3 4.9 fusion.145
  407.3 4.8 multiply_reduce_fusion.7
  412.1 5.3 multiply_convert_fusion.3
  417.4 5.6 fusion.146
  432.9 5.5 fusion.145
  443.3 5.3 multiply_convert_fusion.3
  448.6 5.6 fusion.146
  464.1 5.5 fusion.145
  474.5 5.3 multiply_convert_fusion.3
  479.8 5.6 fusion.146
  495.3 5.5 fusion.145
  505.7 5.3 multiply_convert_fusion.3
  511.0 5.6 fusion.146
  523.3 6.0 convolution_bitcast_fusion.2
  529.4 7.1 fusion.78
  549.9 38.2 %reduce-scatter.11.cloned.1.call-done = f32[512,768]{1,0:T(8,128)} async-done(((f32[2048,768]{1,0:T(8,128)}), f32[512,768]{1,0:T(8,128)}) %reduce-scatter.11.cloned.1.call-update) | async-done | bytes 1572880 | tf_op jit(solution)/shard_map/reduce_scatter | solution.py:237
  590.4 10.2 %all-reduce.2 = (f32[2,768]{1,0:T(2,128)S(1)}, f32[2,768]{1,0:T(2,128)S(1)}, f32[2,768]{1,0:T(2,128)S(1)}) all-reduce(f32[2,768]{1,0:T(2,128)S(1)} %pad_maximum_fusion.1, f32[2,768]{1,0:T(2,128)S(1)} %pad_maximum_fusion.2, f32[2,768]{1,0:T(2,128)S(1)} %pad_maximum_fusion.3), channel_id=1, replica_groups=mesh['dp'=8,'tensor'=4] {'tensor'}, use_global_device_ids=true, to_apply=%region_22.23 | all-reduce | flops 4608 | bytes 36864 | tf_op jit(solution)/shard_map/psum | solution.py:245
  600.7 40.2 %all-reduce = (f32[2,768]{1,0:T(2,128)}, f32[2,768]{1,0:T(2,128)}, f32[2,768]{1,0:T(2,128)}, f32[2,192]{1,0:T(2,128)}, f32[768]{0:T(1024)}) all-reduce(f32[2,768]{1,0:T(2,128)S(1)} %get-tuple-element.288, f32[2,768]{1,0:T(2,128)S(1)} %get-tuple-element.289, ...), channel_id=1, replica_groups=mesh['dp'=8,'tensor'=4] {'dp'}, use_global_device_ids=true, to_apply=%region_23.24 | all-reduce | flops 5760 | bytes 46080 | tf_op jit(solution)/shard_map/psum | solution.py:263
  643.7 182.3 %all-reduce.5.cloned.1.call-done = (f32[3,768,192]{1,2,0:T(8,128)}, f32[192,768]{1,0:T(8,128)}, f32[768,768]{1,0:T(8,128)}, f32[768,768]{1,0:T(8,128)}) async-done(((f32[3,768,192]{1,2,0:T(8,128)}, f32[192,768]{1,0:T(8,128)}, f32[768,768]{1,0:T(8,128)}, f32[768,768]{1,0:T(8,128)}), (f32[3,768,192]{1,2,0:T(8,128)}, f32[192,768]{1,0:T(8,128)}, f32[768,768]{1,0:T(8,128)}, ...) | async-done | bytes 7077904 | tf_op jit(solution)/shard_map/psum | solution.py:263
  (254 shorter events, 177.7 us)
Async XLA Ops:
  7.2 217.1 %copy-start = (bf16[768,768]{1,0:T(8,128)(2,1)S(1)}, bf16[768,768]{1,0:T(8,128)(2,1)}, u32[]{:S(2)}) copy-start(bf16[768,768]{1,0:T(8,128)(2,1)} %param.29) | copy-start | bytes 3538948
  7.2 7.7 copy-start.38
  7.2 37.6 %copy-start.45 = (bf16[3,768,192]{1,2,0:T(8,128)(2,1)S(1)}, bf16[3,768,192]{1,2,0:T(8,128)(2,1)}, u32[]{:S(2)}) copy-start(bf16[3,768,192]{1,2,0:T(8,128)(2,1)} %param.24) | copy-start | bytes 2654212
  7.2 37.6 %all-gather.4.cloned.1.call-start = ((), (), s32[]{:S(2)}) async-start(), calls=%async_computation.4 | async-start | bytes 3932160 | tf_op jit(solution)/shard_map/all_gather | solution.py:152
  8.7 40.0 %copy-start.28 = (f32[512]{0:T(512)}, f32[512]{0:T(512)S(1)}, u32[]{:S(2)}) copy-start(f32[512]{0:T(512)S(1)} %broadcast_multiply_fusion.5) | copy-start | bytes 6148
  10.2 38.5 %copy-start.30 = (f32[512]{0:T(512)}, f32[512]{0:T(512)S(1)}, u32[]{:S(2)}) copy-start(f32[512]{0:T(512)S(1)} %add_rsqrt_fusion.1) | copy-start | bytes 6148
  11.1 37.7 %copy-start.26 = (f32[768]{0:T(1024)}, f32[768]{0:T(1024)S(1)}, u32[]{:S(2)}) copy-start(f32[768]{0:T(1024)S(1)} %get-tuple-element.314) | copy-start | bytes 9220
  13.5 148.2 %reduce-scatter.5.cloned.1.call-start = ((), (), s32[]{:S(2)}) async-start(), calls=%async_computation.5 | async-start | bytes 7864320 | tf_op jit(solution)/shard_map/reduce_scatter | solution.py:163
  95.5 7.1 copy-start.3
  95.5 7.1 copy-start.6
  102.7 91.1 %all-gather.6.cloned.1.call-start = ((), (), s32[]{:S(2)}) async-start(), calls=%async_computation.6 | async-start | bytes 3932160 | tf_op jit(solution)/shard_map/all_gather | solution.py:173
  165.1 59.2 %all-gather.8.cloned.1.call-start = ((), (), s32[]{:S(2)}) async-start(), calls=%async_computation.8 | async-start | bytes 3932160 | tf_op jit(solution)/shard_map/all_gather | solution.py:188
  169.2 140.6 %reduce-scatter.9.cloned.1.call-start = ((), (), s32[]{:S(2)}) async-start(), calls=%async_computation.9 | async-start | bytes 7864320 | tf_op jit(solution)/shard_map/reduce_scatter | solution.py:193
  224.3 22.0 %copy-start.44 = (bf16[768,768]{1,0:T(8,128)(2,1)S(1)}, bf16[768,768]{1,0:T(8,128)(2,1)}, u32[]{:S(2)}) copy-start(bf16[768,768]{1,0:T(8,128)(2,1)} %param.27) | copy-start | bytes 3538948
  250.8 99.3 %reduce-scatter.7.cloned.1.call-start = ((), (), s32[]{:S(2)}) async-start(), calls=%async_computation.7 | async-start | bytes 3932160 | tf_op jit(solution)/shard_map/reduce_scatter | solution.py:179
  262.0 88.1 %copy-start.13 = (bf16[512,768]{1,0:T(8,128)(2,1)S(1)}, bf16[512,768]{1,0:T(8,128)(2,1)}, u32[]{:S(2)}) copy-start(bf16[512,768]{1,0:T(8,128)(2,1)} %get-tuple-element.299) | copy-start | bytes 2359300
  262.0 88.1 %copy-start.32 = (f32[768]{0:T(1024)S(1)}, f32[768]{0:T(1024)}, u32[]{:S(2)}) copy-start(f32[768]{0:T(1024)} %get-tuple-element.235) | copy-start | bytes 9220
  262.0 88.1 %copy-start.41 = (pred[512]{0:T(512)(128)(4,1)S(1)}, pred[512]{0:T(512)(128)(4,1)}, u32[]{:S(2)}) copy-start(pred[512]{0:T(512)(128)(4,1)} %copy-done.40) | copy-start | bytes 1540
  262.1 326.1 %reduce-scatter.11.cloned.1.call-start = ((), (), s32[]{:S(2)}) async-start(), calls=%async_computation.10 | async-start | bytes 7864320 | tf_op jit(solution)/shard_map/reduce_scatter | solution.py:237
  355.1 34.8 %copy-start.25 = (bf16[192,768]{1,0:T(8,128)(2,1)S(1)}, bf16[192,768]{1,0:T(8,128)(2,1)}, u32[]{:S(2)}) copy-start(bf16[192,768]{1,0:T(8,128)(2,1)} %param.26) | copy-start | bytes 884740
  356.7 19.4 %collective-permute-start = (bf16[512,768]{1,0:T(8,128)(2,1)}, bf16[512,768]{1,0:T(8,128)(2,1)S(1)}, u32[]{:S(2)}, u32[]{:S(2)}) collective-permute-start(bf16[512,768]{1,0:T(8,128)(2,1)} %get-tuple-element.301), channel_id=1, source_target_pairs={{0,1},{1,2},{2,3},{3,0},{4,5},{5,6},{6,7},{7,4},{8,9},{9,10},{10,1... | collective-permute-start | bytes 2359304 | tf_op jit(solution)/shard_map/ppermute | solution.py:209
  356.7 20.6 %collective-permute-start.1 = (bf16[512,768]{1,0:T(8,128)(2,1)}, bf16[512,768]{1,0:T(8,128)(2,1)}, u32[]{:S(2)}, u32[]{:S(2)}) collective-permute-start(bf16[512,768]{1,0:T(8,128)(2,1)} %get-tuple-element.301), channel_id=1, source_target_pairs={{0,3},{1,0},{2,1},{3,2},{4,7},{5,4},{6,5},{7,6},{8,11},{9,8},{10,9... | collective-permute-start | bytes 2359304 | tf_op jit(solution)/shard_map/ppermute | solution.py:214
  376.1 11.7 %collective-permute-start.2 = (bf16[512,768]{1,0:T(8,128)(2,1)S(1)}, bf16[512,768]{1,0:T(8,128)(2,1)}, u32[]{:S(2)}, u32[]{:S(2)}) collective-permute-start(bf16[512,768]{1,0:T(8,128)(2,1)S(1)} %collective-permute-done), channel_id=1, source_target_pairs={{0,1},{1,2},{2,3},{3,0},{4,5},{5,6},{6,7},{7,4},{8,9},{9,10},{10,1... | collective-permute-start | bytes 2359304 | tf_op jit(solution)/shard_map/ppermute | solution.py:209
  519.1 10.2 %copy-start.15 = (bf16[2048,3,64]{0,2,1:T(8,128)(2,1)}, bf16[2048,3,64]{0,2,1:T(8,128)(2,1)S(1)}, u32[]{:S(2)}) copy-start(bf16[2048,3,64]{0,2,1:T(8,128)(2,1)S(1)} %convert_element_type.158) | copy-start | bytes 2359300
  529.4 296.7 %all-reduce.5.cloned.1.call-start = ((), (), s32[]{:S(2)}) async-start(), calls=%async_computation.11 | async-start | bytes 14155776 | tf_op jit(solution)/shard_map/psum | solution.py:263
  529.4 7.1 copy-start.20
  548.4 39.8 %copy-start.5 = (bf16[512,768]{1,0:T(8,128)(2,1)S(1)}, bf16[512,768]{1,0:T(8,128)(2,1)}, u32[]{:S(2)}) copy-start(bf16[512,768]{1,0:T(8,128)(2,1)} %param.17) | copy-start | bytes 2359300
  548.4 39.7 %copy-start.27 = (f32[768]{0:T(1024)S(1)}, f32[768]{0:T(1024)}, u32[]{:S(2)}) copy-start(f32[768]{0:T(1024)} %copy-done.26) | copy-start | bytes 9220
  548.4 39.7 %copy-start.29 = (f32[512]{0:T(512)S(1)}, f32[512]{0:T(512)}, u32[]{:S(2)}) copy-start(f32[512]{0:T(512)} %copy-done.28) | copy-start | bytes 6148
  548.4 39.7 %copy-start.31 = (f32[512]{0:T(512)S(1)}, f32[512]{0:T(512)}, u32[]{:S(2)}) copy-start(f32[512]{0:T(512)} %copy-done.30) | copy-start | bytes 6148
  548.5 52.2 %copy-start.39 = (f32[768]{0:T(1024)S(1)}, f32[768]{0:T(1024)}, u32[]{:S(2)}) copy-start(f32[768]{0:T(1024)} %get-tuple-element.291) | copy-start | bytes 9220
  548.5 92.4 %copy-start.8 = (f32[512,768]{1,0:T(8,128)S(1)}, f32[512,768]{1,0:T(8,128)}, u32[]{:S(2)}) copy-start(f32[512,768]{1,0:T(8,128)} %copy-done.7) | copy-start | bytes 4718596
  (36 other events, 95.1 us)
Sparse Core Ops, SparseCore 0:
  13.6 31.2 all-gather.3
  102.8 58.8 reduce-scatter.4
  165.2 28.4 all-gather.5
  195.7 28.4 all-gather.7
  251.0 58.8 reduce-scatter.8
  312.2 37.8 reduce-scatter.6
  529.5 58.6 reduce-scatter.10
  593.7 232.2 all-reduce.4
